TPU v7x, 32 devices: a whole 2x2x4 slice. The times are simulated.
32 devices in a mesh: dp: 4 (over y, x), tm: 2 (over core), space: 4 (over z).
Axes of the slice: x: 2, y: 2, z: 4, core: 2. Of those that a mesh axis runs over, the one named last changes fastest.
Arguments:
- video: bfloat16 [4, 8, 64, 128, 128], P('dp', 'tm', 'space'), may hold values from -6 to 6
- lengths: int32 [4], P('dp'), may hold values from 2 to 8
- norm_gain: float32 [128], replicated, may hold values from 0.25 to 1.75
- norm_shift: float32 [128], replicated, may hold values from -3 to 3
- kernel: bfloat16 [3, 3, 3, 128, 128], replicated, may hold values from -0.109375 to 0.109375
- conv_bias: float32 [128], replicated, may hold values from -3 to 3
- cotangent: bfloat16 [4, 8, 64, 128, 128], P('dp', 'tm', 'space'), may hold values from -0.01171875 to 0.01171875
Outputs:
- output: bfloat16 [4, 8, 64, 128, 128], P('dp', 'tm', 'space')
- grad_kernel: float32 [3, 3, 3, 128, 128], replicated
- grad_bias: float32 [128], replicated
All inputs are finite; a program needn't handle non-finite values.
Results may differ from a plain program's by a relative error of at most 0.0032.
Values may be sent and summed in bfloat16 or wider, within the bound.
No kernel may reach another device: no remote copies, remote signals or barrier semaphores. Data moves between devices by JAX's collectives and lax.ppermute only.
A program may use at most 128 MiB of HBM per device.

v0:
```python
import jax
import jax.numpy as jnp
from jax import lax
from jax.sharding import PartitionSpec as P

GROUPS = 32


def shifted(array, axis, by):
    length = lax.axis_size(axis)
    pairs = [(i, i + by) for i in range(length) if 0 <= i + by < length]
    return lax.ppermute(array, axis, pairs)


def padded_2(block, sides, width):
    for axis, dim in sides:
        count = lax.axis_size(axis)
        forward = [(i, i + 1) for i in range(count - 1)]
        backward = [(target, source) for source, target in forward]
        low = lax.ppermute(
            lax.slice_in_dim(block, block.shape[dim] - width, None, axis=dim), axis, forward
        )
        high = lax.ppermute(lax.slice_in_dim(block, 0, width, axis=dim), axis, backward)
        block = jnp.concatenate([low, block, high], axis=dim)
    return block


def body(video, lengths, norm_gain, norm_shift, kernel, conv_bias, cotangent):
    frames = video.shape[1]
    rows = video.shape[2]
    cols = video.shape[3]
    chans = video.shape[4]
    per = chans // GROUPS
    first = lax.axis_index("tm") * frames
    valid = (first + jnp.arange(frames, dtype=jnp.int32) < lengths[0]).astype(jnp.float32)
    mask = valid[:, None, None, None]
    grouped = video[0].reshape(frames, rows, cols, GROUPS, per)
    gmask = valid[:, None, None, None, None]
    count = lengths[0].astype(jnp.float32) * (rows * lax.axis_size("space")) * cols * per
    local_sum = jnp.sum(grouped * gmask, axis=(0, 1, 2, 4), dtype=jnp.float32)
    mean = lax.psum(local_sum, ("tm", "space")) / count
    spread = (grouped.astype(jnp.float32) - mean[:, None]) * gmask
    variance = lax.psum(jnp.sum(spread * spread, axis=(0, 1, 2, 4)), ("tm", "space")) / count
    normed = (grouped.astype(jnp.float32) - mean[:, None]) * lax.rsqrt(variance + 1e-05)[:, None]
    normed = normed.reshape(frames, rows, cols, chans) * norm_gain + norm_shift
    activated = (jax.nn.silu(normed) * mask).astype(jnp.bfloat16)[None]
    earlier = shifted(activated[:, frames - 2 :], "tm", 1)
    timed = jnp.concatenate([earlier, activated], axis=1)
    extended = padded_2(timed, (("space", 2),), 1)
    padded = jnp.pad(extended[0], ((0, 0), (0, 0), (1, 1), (0, 0)))
    masked = (cotangent[0].astype(jnp.float32) * mask).astype(jnp.bfloat16)
    stacked = jnp.concatenate(
        [
            jnp.pad(masked, ((0, 0), (0, 0), (shift_cols, 2 - shift_cols), (0, 0)))
            for shift_cols in range(3)
        ],
        axis=-1,
    )
    stacked = stacked.reshape(-1, 3 * chans)
    wide_rows = frames * rows * (cols + 2)
    partial_value = jnp.zeros((wide_rows, 3 * chans), jnp.float32)
    grads = []
    for kt in range(3):
        for ky in range(3):
            band = padded[kt : kt + frames, ky : ky + rows].reshape(wide_rows, chans)
            taps = jnp.transpose(kernel[kt, ky], (1, 0, 2)).reshape(chans, 3 * chans)
            partial_value = partial_value + jnp.dot(band, taps, preferred_element_type=jnp.float32)
            product = lax.dot_general(
                band, stacked, (((0,), (0,)), ((), ())), preferred_element_type=jnp.float32
            )
            grads.append(
                jnp.transpose(product.reshape(chans, 3, chans), (1, 0, 2)).reshape(3 * chans, chans)
            )
    partial_value = partial_value.reshape(frames, rows, cols + 2, 3 * chans)
    conv = (
        partial_value[:, :, 0:cols, 0:chans]
        + partial_value[:, :, 1 : cols + 1, chans : 2 * chans]
        + partial_value[:, :, 2 : cols + 2, 2 * chans : 3 * chans]
    )
    output = ((video[0].astype(jnp.float32) + conv + conv_bias) * mask).astype(jnp.bfloat16)[None]
    local_kernel = jnp.concatenate(grads, axis=0)
    local_bias = jnp.sum(masked.reshape(-1, chans).astype(jnp.float32), axis=0)
    summed, grad_bias = lax.psum((local_kernel, local_bias), ("dp", "tm", "space"))
    return (output, summed.reshape(3, 3, 3, chans, chans), grad_bias)


def solution(mesh):
    return jax.shard_map(
        body,
        mesh=mesh,
        in_specs=(
            P("dp", "tm", "space", None, None),
            P("dp"),
            P(),
            P(),
            P(),
            P(),
            P("dp", "tm", "space", None, None),
        ),
        out_specs=(P("dp", "tm", "space", None, None), P(), P()),
        check_vma=False,
    )
```

profile of v0, /device:TPU:0, one launch (start us, length us, event | category | flops | bytes accessed | tf_op | source)
XLA Modules:
  0.0 367.3 jit_solution(12672691524185307099)
XLA Ops:
  11.1 18.5 %psum.28 = f32[32]{0:T(128)S(1)} all-reduce(f32[32]{0:T(128)S(1)} %reduce_sum.36), channel_id=1, replica_groups=mesh['dp'=4,'tm'=2,'space'=4] {'tm','space'}, use_global_device_ids=true, to_apply=%region_2.0 | all-reduce | flops 32 | bytes 256 | tf_op jit(solution)/shard_map/psum | solution.py:41
  29.8 3.3 convert_reduce_fusion
  33.3 13.7 %psum.29 = f32[32]{0:T(128)S(1)} all-reduce(f32[32]{0:T(128)S(1)} %reduce_sum.46), channel_id=1, replica_groups=mesh['dp'=4,'tm'=2,'space'=4] {'tm','space'}, use_global_device_ids=true, to_apply=%region_5.6 | all-reduce | flops 32 | bytes 256 | tf_op jit(solution)/shard_map/psum | solution.py:43
  54.6 3.9 %collective-permute-start.1 = (bf16[1,6,1,128,128]{4,3,2,1,0:T(8,128)(2,1)}, bf16[1,6,1,128,128]{4,3,2,1,0:T(8,128)(2,1)}, u32[]{:S(2)}, u32[]{:S(2)}) collective-permute-start(bf16[1,6,1,128,128]{4,3,2,1,0:T(8,128)(2,1)} %get-tuple-element.14), channel_id=1, source_target_pairs={{0,1},{1,2},{2,3},{4,5},{5,6},{6,7},{8,9},{9,10},{10,11},{12,13},{... | collective-permute-start | bytes 589832 | tf_op jit(solution)/shard_map/ppermute | solution.py:20
  74.0 10.9 %pad_slice_fusion = (bf16[4,16,130,128]{3,2,1,0:T(8,128)(2,1)}, bf16[4,16,130,128]{3,2,1,0:T(8,128)(2,1)}, bf16[4,16,130,128]{3,2,1,0:T(8,128)(2,1)}, bf16[4,16,...) fusion(bf16[6,18,128,128]{3,2,1,0:T(8,128)(2,1)S(1)} %maximum_b, ...), kind=kLoop, calls=%fused_computation.67 | loop fusion | bytes 22708224 | tf_op jit(solution)/shard_map/slice | solution.py:65
  84.9 4.1 %reshape.166 = bf16[8320,128]{1,0:T(8,128)(2,1)} reshape(bf16[4,16,130,128]{3,2,1,0:T(8,128)(2,1)} %get-tuple-element.5) | data formatting | bytes 4259840 | tf_op jit(solution)/shard_map/reshape | solution.py:65
  89.0 4.0 %reshape.152 = bf16[8320,128]{1,0:T(8,128)(2,1)} reshape(bf16[4,16,130,128]{3,2,1,0:T(8,128)(2,1)} %get-tuple-element.6) | data formatting | bytes 4259840 | tf_op jit(solution)/shard_map/reshape | solution.py:65
  93.0 4.0 %reshape.154 = bf16[8320,128]{1,0:T(8,128)(2,1)} reshape(bf16[4,16,130,128]{3,2,1,0:T(8,128)(2,1)} %get-tuple-element.7) | data formatting | bytes 4259840 | tf_op jit(solution)/shard_map/reshape | solution.py:65
  97.0 4.0 %reshape.156 = bf16[8320,128]{1,0:T(8,128)(2,1)} reshape(bf16[4,16,130,128]{3,2,1,0:T(8,128)(2,1)} %get-tuple-element.8) | data formatting | bytes 4259840 | tf_op jit(solution)/shard_map/reshape | solution.py:65
  101.1 4.0 %reshape.158 = bf16[8320,128]{1,0:T(8,128)(2,1)} reshape(bf16[4,16,130,128]{3,2,1,0:T(8,128)(2,1)} %get-tuple-element.9) | data formatting | bytes 4259840 | tf_op jit(solution)/shard_map/reshape | solution.py:65
  105.1 4.1 %reshape.160 = bf16[8320,128]{1,0:T(8,128)(2,1)} reshape(bf16[4,16,130,128]{3,2,1,0:T(8,128)(2,1)} %get-tuple-element.10) | data formatting | bytes 4259840 | tf_op jit(solution)/shard_map/reshape | solution.py:65
  109.2 4.0 %reshape.162 = bf16[8320,128]{1,0:T(8,128)(2,1)} reshape(bf16[4,16,130,128]{3,2,1,0:T(8,128)(2,1)} %get-tuple-element.11) | data formatting | bytes 4259840 | tf_op jit(solution)/shard_map/reshape | solution.py:65
  113.3 4.0 %reshape.164 = bf16[8320,128]{1,0:T(8,128)(2,1)} reshape(bf16[4,16,130,128]{3,2,1,0:T(8,128)(2,1)} %get-tuple-element.12) | data formatting | bytes 4259840 | tf_op jit(solution)/shard_map/reshape | solution.py:65
  117.3 4.1 %reshape.150 = bf16[8320,128]{1,0:T(8,128)(2,1)} reshape(bf16[4,16,130,128]{3,2,1,0:T(8,128)(2,1)} %get-tuple-element.13) | data formatting | bytes 4259840 | tf_op jit(solution)/shard_map/reshape | solution.py:65
  121.4 3.4 fusion.47
  124.9 3.6 convolution_add_fusion.7
  128.5 3.6 convolution_add_fusion.6
  132.1 3.6 convolution_add_fusion.5
  135.7 3.6 convolution_add_fusion.4
  139.3 3.6 convolution_add_fusion.3
  143.0 3.6 convolution_add_fusion.2
  146.6 3.8 %convolution_add_fusion.1 = f32[8320,384]{1,0:T(8,128)S(1)} fusion(f32[8320,384]{1,0:T(8,128)S(1)} %convolution_add_fusion.2, bf16[8320,128]{1,0:T(8,128)(2,1)} %reshape.164, bf16[128,384]{0,1:T(8,128)(2,1)S(1)} %bitcast.176), kind=kOutput, calls=%fused_computation.3 | convolution fusion | flops 821084160 | bytes 27787264 | tf_op jit(solution)/shard_map/dot_general | solution.py:67
  150.4 8.2 %convolution_add_fusion = f32[8320,384]{1,0:T(8,128)} fusion(f32[8320,384]{1,0:T(8,128)S(1)} %convolution_add_fusion.1, bf16[8320,128]{1,0:T(8,128)(2,1)} %reshape.166, bf16[128,384]{0,1:T(8,128)(2,1)S(1)} %bitcast.175), kind=kOutput, calls=%fused_computation.2 | convolution fusion | flops 821084160 | bytes 27787264 | tf_op jit(solution)/shard_map/dot_general | solution.py:67
  158.6 12.0 %reshape.168 = f32[4,16,130,384]{3,2,1,0:T(8,128)} reshape(f32[8320,384]{1,0:T(8,128)} %convolution_add_fusion) | data formatting | bytes 25559040 | tf_op jit(solution)/shard_map/reshape | solution.py:74
  170.6 7.8 %fusion.20 = (bf16[4,16,128,128]{3,2,1,0:T(8,128)(2,1)S(1)}, bf16[1,4,16,128,128]{4,3,2,1,0:T(8,128)(2,1)}) fusion(bf16[1,4,16,128,128]{4,3,2,1,0:T(8,128)(2,1)} %param.13, f32[4]{0:T(128)S(1)} %compare_convert_fusion, f32[128]{0:T(128)S(1)} %copy-done.23, f32[4,16,130,384]{3,2,1,0:T(8,128)} %reshape.168, bf16[1,4,16,128,128]{4,3,2,1,0:T(8,128)(2,1)S(1)} %copy-done.1), kind=kLoop, calls=%fused_computation.37 | loop fusion | flops 10485760 | bytes 20972048 | tf_op jit(solution)/shard_map/convert_element_type | solution.py:51
  178.4 3.9 %fusion.5 = bf16[4,16,130,384]{3,2,1,0:T(8,128)(2,1)} fusion(bf16[4,16,128,128]{3,2,1,0:T(8,128)(2,1)S(1)} %get-tuple-element.25), kind=kLoop, calls=%fused_computation.17 | loop fusion | flops 44728320 | bytes 8486912 | tf_op jit(solution)/shard_map/concatenate | solution.py:52
  182.4 8.5 %reshape.169 = bf16[8320,384]{1,0:T(8,128)(2,1)} reshape(bf16[4,16,130,384]{3,2,1,0:T(8,128)(2,1)} %fusion.5) | data formatting | bytes 12779520 | tf_op jit(solution)/shard_map/reshape | solution.py:59
  190.9 9.4 %copy.29 = bf16[384,8320]{1,0:T(8,128)(2,1)} copy(bf16[384,8320]{0,1:T(8,128)(2,1)} %bitcast.163) | data formatting | bytes 12779520 | tf_op jit(solution)/shard_map/dot_general | solution.py:68
  200.3 4.9 %fusion.27 = f32[128,3,128]{2,0,1:T(8,128)S(1)} fusion(bf16[3,128,8320]{2,1,0:T(8,128)(2,1)} %bitcast.154, bf16[8320,128]{1,0:T(8,128)(2,1)S(1)} %copy-done.5), kind=kOutput, calls=%fused_computation.48 | convolution fusion | flops 817889280 | bytes 8716288 | tf_op jit(solution)/shard_map/dot_general | solution.py:68
  223.1 41.4 %psum.31 = f32[128]{0:T(128)} all-reduce(f32[128]{0:T(128)S(1)} %copy-done.24), channel_id=1, replica_groups=mesh['dp'=4,'tm'=2,'space'=4] {'dp','tm','space'}, use_global_device_ids=true, to_apply=%region_8.9 | all-reduce | flops 128 | bytes 1024 | tf_op jit(solution)/shard_map/psum | solution.py:83
  264.5 92.7 %all-reduce.6.cloned.1.call-done = f32[3,3,3,128,128]{4,3,2,1,0:T(8,128)} async-done(((f32[3,3,3,128,128]{4,3,2,1,0:T(8,128)}), f32[3,3,3,128,128]{4,3,2,1,0:T(8,128)}) %all-reduce.6.cloned.1.call-update) | async-done | bytes 1769488 | tf_op jit(solution)/shard_map/psum | solution.py:83
  357.2 2.9 copy.76
  (100 shorter events, 44.0 us)
Async XLA Ops:
  7.2 22.6 %copy-start.1 = (bf16[1,4,16,128,128]{4,3,2,1,0:T(8,128)(2,1)S(1)}, bf16[1,4,16,128,128]{4,3,2,1,0:T(8,128)(2,1)}, u32[]{:S(2)}) copy-start(bf16[1,4,16,128,128]{4,3,2,1,0:T(8,128)(2,1)} %param.7) | copy-start | bytes 6291460
  7.2 40.0 %copy-start.21 = (f32[128]{0:T(128)S(1)}, f32[128]{0:T(128)}, u32[]{:S(2)}) copy-start(f32[128]{0:T(128)} %param.10) | copy-start | bytes 1540
  7.2 40.0 %copy-start.22 = (f32[128]{0:T(128)S(1)}, f32[128]{0:T(128)}, u32[]{:S(2)}) copy-start(f32[128]{0:T(128)} %param.9) | copy-start | bytes 1540
  7.2 350.0 %all-reduce.6.cloned.1.call-start = ((), (), s32[]{:S(2)}) async-start(), calls=%async_computation | async-start | bytes 3538944 | tf_op jit(solution)/shard_map/psum | solution.py:83
  48.9 12.3 %copy-start.10 = (bf16[1,4,16,128,128]{4,3,2,1,0:T(8,128)(2,1)}, bf16[1,4,16,128,128]{4,3,2,1,0:T(8,128)(2,1)S(1)}, u32[]{:S(2)}) copy-start(bf16[1,4,16,128,128]{4,3,2,1,0:T(8,128)(2,1)S(1)} %fusion.18) | copy-start | bytes 6291460
  48.9 11.4 %copy-start.13 = (bf16[3,3,3,128,128]{4,3,2,1,0:T(8,128)(2,1)S(1)}, bf16[3,3,3,128,128]{4,3,2,1,0:T(8,128)(2,1)}, u32[]{:S(2)}) copy-start(bf16[3,3,3,128,128]{4,3,2,1,0:T(8,128)(2,1)} %param.11) | copy-start | bytes 2654212
  49.0 4.8 %collective-permute-start = (bf16[1,2,16,128,128]{4,3,2,1,0:T(8,128)(2,1)S(1)}, bf16[1,2,16,128,128]{4,3,2,1,0:T(8,128)(2,1)S(1)}, u32[]{:S(2)}, u32[]{:S(2)}) collective-permute-start(bf16[1,2,16,128,128]{4,3,2,1,0:T(8,128)(2,1)S(1)} %slice.96), channel_id=1, source_target_pairs={{0,4},{1,5},{2,6},{3,7},{8,12},{9,13},{10,14},{11,15},{16,20},{17,... | collective-permute-start | bytes 3145736 | tf_op jit(solution)/shard_map/ppermute | solution.py:12
  54.6 17.3 %collective-permute-start.1 = (bf16[1,6,1,128,128]{4,3,2,1,0:T(8,128)(2,1)}, bf16[1,6,1,128,128]{4,3,2,1,0:T(8,128)(2,1)}, u32[]{:S(2)}, u32[]{:S(2)}) collective-permute-start(bf16[1,6,1,128,128]{4,3,2,1,0:T(8,128)(2,1)} %get-tuple-element.14), channel_id=1, source_target_pairs={{0,1},{1,2},{2,3},{4,5},{5,6},{6,7},{8,9},{9,10},{10,11},{12,13},{... | collective-permute-start | bytes 589832 | tf_op jit(solution)/shard_map/ppermute | solution.py:20
  58.5 13.4 %collective-permute-start.2 = (bf16[1,6,1,128,128]{4,3,2,1,0:T(8,128)(2,1)}, bf16[1,6,1,128,128]{4,3,2,1,0:T(8,128)(2,1)}, u32[]{:S(2)}, u32[]{:S(2)}) collective-permute-start(bf16[1,6,1,128,128]{4,3,2,1,0:T(8,128)(2,1)} %get-tuple-element.15), channel_id=1, source_target_pairs={{1,0},{2,1},{3,2},{5,4},{6,5},{7,6},{9,8},{10,9},{11,10},{13,12},{... | collective-permute-start | bytes 589832 | tf_op jit(solution)/shard_map/ppermute | solution.py:23
  124.9 3.6 copy-start.20
  128.5 3.6 copy-start.19
  132.1 3.6 copy-start.18
  135.7 3.6 copy-start.17
  139.3 3.6 copy-start.16
  143.0 3.6 copy-start.15
  146.6 3.8 %copy-start.14 = (bf16[1,1,3,128,128]{3,4,2,1,0:T(8,128)(2,1)S(1)}, bf16[1,1,3,128,128]{3,4,2,1,0:T(8,128)(2,1)}, u32[]{:S(2)}) copy-start(bf16[1,1,3,128,128]{3,4,2,1,0:T(8,128)(2,1)} %copy.65) | copy-start | bytes 294916
  158.6 12.0 %copy-start.23 = (f32[128]{0:T(128)S(1)}, f32[128]{0:T(128)}, u32[]{:S(2)}) copy-start(f32[128]{0:T(128)} %param.12) | copy-start | bytes 1540
  190.9 9.4 %copy-start.5 = (bf16[8320,128]{1,0:T(8,128)(2,1)S(1)}, bf16[8320,128]{1,0:T(8,128)(2,1)}, u32[]{:S(2)}) copy-start(bf16[8320,128]{1,0:T(8,128)(2,1)} %reshape.166) | copy-start | bytes 6389764
  200.3 5.0 %copy-start = (bf16[384,8320]{1,0:T(8,128)(2,1)S(1)}, bf16[384,8320]{1,0:T(8,128)(2,1)}, u32[]{:S(2)}) copy-start(bf16[384,8320]{1,0:T(8,128)(2,1)} %copy.29) | copy-start | bytes 19169284
  200.3 5.3 %copy-start.9 = (bf16[8320,128]{1,0:T(8,128)(2,1)S(1)}, bf16[8320,128]{1,0:T(8,128)(2,1)}, u32[]{:S(2)}) copy-start(bf16[8320,128]{1,0:T(8,128)(2,1)} %reshape.164) | copy-start | bytes 6389764
  205.6 2.0 copy-start.8
  207.6 2.0 copy-start.7
  209.6 2.0 copy-start.6
  211.6 2.0 copy-start.4
  213.6 2.0 copy-start.3
  215.6 2.0 copy-start.2
  217.7 2.0 copy-start.11
  221.7 1.5 copy-start.24
  221.9 1.2 copy-start.12
Sparse Core Ops, SparseCore 0:
  223.2 133.9 all-reduce.5
where the time goes:
time: 373 us; the launch traced here: 367 us
  waiting for transfers between devices  94.9 us (25%)
  local copies, waits for them, and re-layouts  94.3 us (25%)
  blocking collectives  73.7 us (20%)
  matrix products  57.8 us (15%)
  other arithmetic  22.5 us (6%)
  between operations  15.8 us (4%)
  starting transfers between devices  8.35 us (2%)
    psum x1, waiting for transfers between devices, body(): lax.psum((local_kernel, local_bias), ('dp', 'tm', 'space'))  92.7 us
    psum x1, blocking collectives, body(): lax.psum((local_kernel, local_bias), ('dp', 'tm', 'space'))  41.4 us
    dot_general x9, matrix products, body(): jnp.dot(band, taps, preferred_element_type=jnp.float32)  37 us
    reshape x9, local copies, waits for them, and re-layouts, body(): band = padded[kt:kt + frames, ky:ky + rows].reshape(wide_rows, chans)  36.5 us
    dot_general x9, matrix products, body(): lax.dot_general(band, stacked, (((0,), (0,)), ((), ())), preferred_elemen...  20.8 us
    psum x1, blocking collectives, body(): mean = lax.psum(local_sum, ('tm', 'space')) / count  18.5 us
    unnamed x68, local copies, waits for them, and re-layouts  15.4 us
    psum x1, blocking collectives, body(): lax.psum(jnp.sum(spread * spread, axis=(0, 1, 2, 4)), ('tm', 'space'))  13.7 us
  transfers between devices with their start and end apart: 4, of which 2 were waited for; matrix products, arithmetic and copies ran while one was open for 3% of the time, Pallas kernels for 0%

commit v1 on v0

--- a/solution.py
+++ b/solution.py
@@ -1,9 +1,18 @@
+import functools
 import jax
 import jax.numpy as jnp
 from jax import lax
 from jax.sharding import PartitionSpec as P
 
 GROUPS = 32
+
+
+def save_stocks(z_in, mesh_ax, group_axis):
+    current_value = jax.lax.psum(jax.lax.psum(z_in, axis_name=group_axis), axis_name=mesh_ax)
+    return current_value
+
+
+assign_screen = functools.partial(save_stocks, mesh_ax="dp", group_axis=("tm", "space"))
 
 
 def shifted(array, axis, by):
@@ -80,7 +89,7 @@
     output = ((video[0].astype(jnp.float32) + conv + conv_bias) * mask).astype(jnp.bfloat16)[None]
     local_kernel = jnp.concatenate(grads, axis=0)
     local_bias = jnp.sum(masked.reshape(-1, chans).astype(jnp.float32), axis=0)
-    summed, grad_bias = lax.psum((local_kernel, local_bias), ("dp", "tm", "space"))
+    summed, grad_bias = assign_screen((local_kernel, local_bias))
     return (output, summed.reshape(3, 3, 3, chans, chans), grad_bias)
 
 

time: 373 us -> 370 us (level)
  blocking collectives: 73.7 us -> 43.1 us
  waiting for transfers between devices: 94.9 us -> 122 us
    psum x1, blocking collectives: 41.4 us -> 10.3 us  [save_stocks(): jax.lax.psum(jax.lax.psum(z_in, axis_name=group_axis), axis_name=mesh_ax)]
    psum x1 -> x2, waiting for transfers between devices: 92.7 us -> 120 us  [the longest x1 64.1 us: save_stocks(): jax.lax.psum(z_in, axis_name=group_axis)]
  transfers between devices with their start and end apart: 4 -> 5, of which waited for: 2 -> 3; matrix products, arithmetic and copies ran while one was open for 3% -> 3% of each run, Pallas kernels for 0% -> 0%
where the time goes in v1:
time: 370 us; the launch traced here: 364 us
  waiting for transfers between devices  122 us (33%)
  local copies, waits for them, and re-layouts  94.3 us (25%)
  matrix products  57.8 us (16%)
  blocking collectives  43.1 us (12%)
  other arithmetic  22 us (6%)
  between operations  15.8 us (4%)
  starting transfers between devices  8.4 us (2%)
    psum x1, waiting for transfers between devices, save_stocks(): jax.lax.psum(z_in, axis_name=group_axis)  64.1 us
    psum x1, waiting for transfers between devices, save_stocks(): jax.lax.psum(jax.lax.psum(z_in, axis_name=group_axis), axis_name=mesh_ax)  56.1 us
    dot_general x9, matrix products, body(): jnp.dot(band, taps, preferred_element_type=jnp.float32)  37 us
    reshape x9, local copies, waits for them, and re-layouts, body(): band = padded[kt:kt + frames, ky:ky + rows].reshape(wide_rows, chans)  36.6 us
    dot_general x9, matrix products, body(): lax.dot_general(band, stacked, (((0,), (0,)), ((), ())), preferred_elemen...  20.8 us
    psum x1, blocking collectives, body(): mean = lax.psum(local_sum, ('tm', 'space')) / count  18.5 us
    unnamed x68, local copies, waits for them, and re-layouts  15.5 us
    psum x1, blocking collectives, body(): lax.psum(jnp.sum(spread * spread, axis=(0, 1, 2, 4)), ('tm', 'space'))  14.2 us
  transfers between devices with their start and end apart: 5, of which 3 were waited for; matrix products, arithmetic and copies ran while one was open for 3% of the time, Pallas kernels for 0%

profile of v1, /device:TPU:0, one launch (start us, length us, event | category | flops | bytes accessed | tf_op | source)
XLA Modules:
  0.0 364.0 jit_solution(14880789963227678747)
XLA Ops:
  11.1 18.5 %psum.42 = f32[32]{0:T(128)S(1)} all-reduce(f32[32]{0:T(128)S(1)} %reduce_sum.36), channel_id=1, replica_groups=mesh['dp'=4,'tm'=2,'space'=4] {'tm','space'}, use_global_device_ids=true, to_apply=%region_2.0 | all-reduce | flops 32 | bytes 256 | tf_op jit(solution)/shard_map/psum | solution.py:50
  32.8 14.2 %all-reduce.4 = (f32[32]{0:T(128)S(1)}, f32[128]{0:T(128)}) all-reduce(f32[32]{0:T(128)S(1)} %reduce_sum.46, f32[128]{0:T(128)S(1)} %get-tuple-element.3), channel_id=1, replica_groups=mesh['dp'=4,'tm'=2,'space'=4] {'tm','space'}, use_global_device_ids=true, to_apply=%region_5.6 | all-reduce | flops 160 | bytes 1280 | tf_op jit(solution)/shard_map/psum | solution.py:52
  54.6 3.9 %collective-permute-start.1 = (bf16[1,6,1,128,128]{4,3,2,1,0:T(8,128)(2,1)}, bf16[1,6,1,128,128]{4,3,2,1,0:T(8,128)(2,1)}, u32[]{:S(2)}, u32[]{:S(2)}) collective-permute-start(bf16[1,6,1,128,128]{4,3,2,1,0:T(8,128)(2,1)} %get-tuple-element.16), channel_id=1, source_target_pairs={{0,1},{1,2},{2,3},{4,5},{5,6},{6,7},{8,9},{9,10},{10,11},{12,13},{... | collective-permute-start | bytes 589832 | tf_op jit(solution)/shard_map/ppermute | solution.py:29
  74.0 10.9 %pad_slice_fusion = (bf16[4,16,130,128]{3,2,1,0:T(8,128)(2,1)}, bf16[4,16,130,128]{3,2,1,0:T(8,128)(2,1)}, bf16[4,16,130,128]{3,2,1,0:T(8,128)(2,1)}, bf16[4,16,...) fusion(bf16[6,18,128,128]{3,2,1,0:T(8,128)(2,1)S(1)} %maximum_b, ...), kind=kLoop, calls=%fused_computation.67 | loop fusion | bytes 22708224 | tf_op jit(solution)/shard_map/slice | solution.py:74
  84.9 4.1 %reshape.166 = bf16[8320,128]{1,0:T(8,128)(2,1)} reshape(bf16[4,16,130,128]{3,2,1,0:T(8,128)(2,1)} %get-tuple-element.7) | data formatting | bytes 4259840 | tf_op jit(solution)/shard_map/reshape | solution.py:74
  89.0 4.0 %reshape.152 = bf16[8320,128]{1,0:T(8,128)(2,1)} reshape(bf16[4,16,130,128]{3,2,1,0:T(8,128)(2,1)} %get-tuple-element.8) | data formatting | bytes 4259840 | tf_op jit(solution)/shard_map/reshape | solution.py:74
  93.0 4.1 %reshape.154 = bf16[8320,128]{1,0:T(8,128)(2,1)} reshape(bf16[4,16,130,128]{3,2,1,0:T(8,128)(2,1)} %get-tuple-element.9) | data formatting | bytes 4259840 | tf_op jit(solution)/shard_map/reshape | solution.py:74
  97.1 4.1 %reshape.156 = bf16[8320,128]{1,0:T(8,128)(2,1)} reshape(bf16[4,16,130,128]{3,2,1,0:T(8,128)(2,1)} %get-tuple-element.10) | data formatting | bytes 4259840 | tf_op jit(solution)/shard_map/reshape | solution.py:74
  101.1 4.1 %reshape.158 = bf16[8320,128]{1,0:T(8,128)(2,1)} reshape(bf16[4,16,130,128]{3,2,1,0:T(8,128)(2,1)} %get-tuple-element.11) | data formatting | bytes 4259840 | tf_op jit(solution)/shard_map/reshape | solution.py:74
  105.2 4.1 %reshape.160 = bf16[8320,128]{1,0:T(8,128)(2,1)} reshape(bf16[4,16,130,128]{3,2,1,0:T(8,128)(2,1)} %get-tuple-element.12) | data formatting | bytes 4259840 | tf_op jit(solution)/shard_map/reshape | solution.py:74
  109.3 4.0 %reshape.162 = bf16[8320,128]{1,0:T(8,128)(2,1)} reshape(bf16[4,16,130,128]{3,2,1,0:T(8,128)(2,1)} %get-tuple-element.13) | data formatting | bytes 4259840 | tf_op jit(solution)/shard_map/reshape | solution.py:74
  113.3 4.0 %reshape.164 = bf16[8320,128]{1,0:T(8,128)(2,1)} reshape(bf16[4,16,130,128]{3,2,1,0:T(8,128)(2,1)} %get-tuple-element.14) | data formatting | bytes 4259840 | tf_op jit(solution)/shard_map/reshape | solution.py:74
  117.4 4.2 %reshape.150 = bf16[8320,128]{1,0:T(8,128)(2,1)} reshape(bf16[4,16,130,128]{3,2,1,0:T(8,128)(2,1)} %get-tuple-element.15) | data formatting | bytes 4259840 | tf_op jit(solution)/shard_map/reshape | solution.py:74
  121.5 3.4 fusion.47
  125.0 3.6 convolution_add_fusion.7
  128.6 3.6 convolution_add_fusion.6
  132.2 3.6 convolution_add_fusion.5
  135.8 3.6 convolution_add_fusion.4
  139.4 3.6 convolution_add_fusion.3
  143.1 3.6 convolution_add_fusion.2
  146.7 3.8 %convolution_add_fusion.1 = f32[8320,384]{1,0:T(8,128)S(1)} fusion(f32[8320,384]{1,0:T(8,128)S(1)} %convolution_add_fusion.2, bf16[8320,128]{1,0:T(8,128)(2,1)} %reshape.164, bf16[128,384]{0,1:T(8,128)(2,1)S(1)} %bitcast.176), kind=kOutput, calls=%fused_computation.3 | convolution fusion | flops 821084160 | bytes 27787264 | tf_op jit(solution)/shard_map/dot_general | solution.py:76
  150.5 8.2 %convolution_add_fusion = f32[8320,384]{1,0:T(8,128)} fusion(f32[8320,384]{1,0:T(8,128)S(1)} %convolution_add_fusion.1, bf16[8320,128]{1,0:T(8,128)(2,1)} %reshape.166, bf16[128,384]{0,1:T(8,128)(2,1)S(1)} %bitcast.175), kind=kOutput, calls=%fused_computation.2 | convolution fusion | flops 821084160 | bytes 27787264 | tf_op jit(solution)/shard_map/dot_general | solution.py:76
  158.7 12.0 %reshape.168 = f32[4,16,130,384]{3,2,1,0:T(8,128)} reshape(f32[8320,384]{1,0:T(8,128)} %convolution_add_fusion) | data formatting | bytes 25559040 | tf_op jit(solution)/shard_map/reshape | solution.py:83
  170.7 7.8 %fusion.20 = (bf16[4,16,128,128]{3,2,1,0:T(8,128)(2,1)S(1)}, bf16[1,4,16,128,128]{4,3,2,1,0:T(8,128)(2,1)}) fusion(bf16[1,4,16,128,128]{4,3,2,1,0:T(8,128)(2,1)} %param.13, f32[4]{0:T(128)S(1)} %compare_convert_fusion, f32[128]{0:T(128)S(1)} %copy-done.23, f32[4,16,130,384]{3,2,1,0:T(8,128)} %reshape.168, bf16[1,4,16,128,128]{4,3,2,1,0:T(8,128)(2,1)S(1)} %copy-done.1), kind=kLoop, calls=%fused_computation.37 | loop fusion | flops 10485760 | bytes 20972048 | tf_op jit(solution)/shard_map/convert_element_type | solution.py:60
  178.6 3.9 %fusion.5 = bf16[4,16,130,384]{3,2,1,0:T(8,128)(2,1)} fusion(bf16[4,16,128,128]{3,2,1,0:T(8,128)(2,1)S(1)} %get-tuple-element.27), kind=kLoop, calls=%fused_computation.17 | loop fusion | flops 44728320 | bytes 8486912 | tf_op jit(solution)/shard_map/concatenate | solution.py:61
  182.5 8.5 %reshape.169 = bf16[8320,384]{1,0:T(8,128)(2,1)} reshape(bf16[4,16,130,384]{3,2,1,0:T(8,128)(2,1)} %fusion.5) | data formatting | bytes 12779520 | tf_op jit(solution)/shard_map/reshape | solution.py:68
  191.0 9.4 %copy.29 = bf16[384,8320]{1,0:T(8,128)(2,1)} copy(bf16[384,8320]{0,1:T(8,128)(2,1)} %bitcast.163) | data formatting | bytes 12779520 | tf_op jit(solution)/shard_map/dot_general | solution.py:77
  200.4 4.9 %fusion.27 = f32[128,3,128]{2,0,1:T(8,128)S(1)} fusion(bf16[3,128,8320]{2,1,0:T(8,128)(2,1)} %bitcast.154, bf16[8320,128]{1,0:T(8,128)(2,1)S(1)} %copy-done.5), kind=kOutput, calls=%fused_computation.48 | convolution fusion | flops 817889280 | bytes 8716288 | tf_op jit(solution)/shard_map/dot_general | solution.py:77
  223.3 64.1 %all-reduce.8.cloned.1.call-done = f32[3456,128]{1,0:T(8,128)} async-done(((f32[3456,128]{1,0:T(8,128)}), f32[3456,128]{1,0:T(8,128)}) %all-reduce.8.cloned.1.call-update) | async-done | bytes 1769488 | tf_op jit(solution)/shard_map/psum | solution.py:11
  287.4 10.3 %psum.47 = f32[128]{0:T(128)} all-reduce(f32[128]{0:T(128)S(1)} %copy-done.24), channel_id=1, replica_groups=mesh['dp'=4,'tm'=2,'space'=4] {'dp'}, use_global_device_ids=true, to_apply=%region_10.11 | all-reduce | flops 128 | bytes 1024 | tf_op jit(solution)/shard_map/psum | solution.py:11
  297.8 56.1 %all-reduce.10.cloned.1.call-done = f32[3,3,3,128,128]{4,3,2,1,0:T(8,128)} async-done(((f32[3,3,3,128,128]{4,3,2,1,0:T(8,128)}), f32[3,3,3,128,128]{4,3,2,1,0:T(8,128)}) %all-reduce.10.cloned.1.call-update) | async-done | bytes 1769488 | tf_op jit(solution)/shard_map/psum | solution.py:11
  353.9 2.9 copy.77
  (103 shorter events, 46.9 us)
Async XLA Ops:
  7.2 22.6 %copy-start.1 = (bf16[1,4,16,128,128]{4,3,2,1,0:T(8,128)(2,1)S(1)}, bf16[1,4,16,128,128]{4,3,2,1,0:T(8,128)(2,1)}, u32[]{:S(2)}) copy-start(bf16[1,4,16,128,128]{4,3,2,1,0:T(8,128)(2,1)} %param.7) | copy-start | bytes 6291460
  7.2 40.0 %copy-start.21 = (f32[128]{0:T(128)S(1)}, f32[128]{0:T(128)}, u32[]{:S(2)}) copy-start(f32[128]{0:T(128)} %param.10) | copy-start | bytes 1540
  7.2 40.0 %copy-start.22 = (f32[128]{0:T(128)S(1)}, f32[128]{0:T(128)}, u32[]{:S(2)}) copy-start(f32[128]{0:T(128)} %param.9) | copy-start | bytes 1540
  7.2 280.2 %all-reduce.8.cloned.1.call-start = ((), (), s32[]{:S(2)}) async-start(), calls=%async_computation | async-start | bytes 3538944 | tf_op jit(solution)/shard_map/psum | solution.py:11
  48.9 12.3 %copy-start.10 = (bf16[1,4,16,128,128]{4,3,2,1,0:T(8,128)(2,1)}, bf16[1,4,16,128,128]{4,3,2,1,0:T(8,128)(2,1)S(1)}, u32[]{:S(2)}) copy-start(bf16[1,4,16,128,128]{4,3,2,1,0:T(8,128)(2,1)S(1)} %fusion.18) | copy-start | bytes 6291460
  48.9 11.4 %copy-start.13 = (bf16[3,3,3,128,128]{4,3,2,1,0:T(8,128)(2,1)S(1)}, bf16[3,3,3,128,128]{4,3,2,1,0:T(8,128)(2,1)}, u32[]{:S(2)}) copy-start(bf16[3,3,3,128,128]{4,3,2,1,0:T(8,128)(2,1)} %param.11) | copy-start | bytes 2654212
  49.0 4.8 %collective-permute-start = (bf16[1,2,16,128,128]{4,3,2,1,0:T(8,128)(2,1)S(1)}, bf16[1,2,16,128,128]{4,3,2,1,0:T(8,128)(2,1)S(1)}, u32[]{:S(2)}, u32[]{:S(2)}) collective-permute-start(bf16[1,2,16,128,128]{4,3,2,1,0:T(8,128)(2,1)S(1)} %slice.96), channel_id=1, source_target_pairs={{0,4},{1,5},{2,6},{3,7},{8,12},{9,13},{10,14},{11,15},{16,20},{17,... | collective-permute-start | bytes 3145736 | tf_op jit(solution)/shard_map/ppermute | solution.py:21
  54.6 17.4 %collective-permute-start.1 = (bf16[1,6,1,128,128]{4,3,2,1,0:T(8,128)(2,1)}, bf16[1,6,1,128,128]{4,3,2,1,0:T(8,128)(2,1)}, u32[]{:S(2)}, u32[]{:S(2)}) collective-permute-start(bf16[1,6,1,128,128]{4,3,2,1,0:T(8,128)(2,1)} %get-tuple-element.16), channel_id=1, source_target_pairs={{0,1},{1,2},{2,3},{4,5},{5,6},{6,7},{8,9},{9,10},{10,11},{12,13},{... | collective-permute-start | bytes 589832 | tf_op jit(solution)/shard_map/ppermute | solution.py:29
  58.6 13.5 %collective-permute-start.2 = (bf16[1,6,1,128,128]{4,3,2,1,0:T(8,128)(2,1)}, bf16[1,6,1,128,128]{4,3,2,1,0:T(8,128)(2,1)}, u32[]{:S(2)}, u32[]{:S(2)}) collective-permute-start(bf16[1,6,1,128,128]{4,3,2,1,0:T(8,128)(2,1)} %get-tuple-element.17), channel_id=1, source_target_pairs={{1,0},{2,1},{3,2},{5,4},{6,5},{7,6},{9,8},{10,9},{11,10},{13,12},{... | collective-permute-start | bytes 589832 | tf_op jit(solution)/shard_map/ppermute | solution.py:32
  125.0 3.6 copy-start.20
  128.6 3.6 copy-start.19
  132.2 3.6 copy-start.18
  135.8 3.6 copy-start.17
  139.4 3.6 copy-start.16
  143.1 3.6 copy-start.15
  146.7 3.8 %copy-start.14 = (bf16[1,1,3,128,128]{3,4,2,1,0:T(8,128)(2,1)S(1)}, bf16[1,1,3,128,128]{3,4,2,1,0:T(8,128)(2,1)}, u32[]{:S(2)}) copy-start(bf16[1,1,3,128,128]{3,4,2,1,0:T(8,128)(2,1)} %copy.65) | copy-start | bytes 294916
  158.7 12.0 %copy-start.23 = (f32[128]{0:T(128)S(1)}, f32[128]{0:T(128)}, u32[]{:S(2)}) copy-start(f32[128]{0:T(128)} %param.12) | copy-start | bytes 1540
  191.0 9.4 %copy-start.5 = (bf16[8320,128]{1,0:T(8,128)(2,1)S(1)}, bf16[8320,128]{1,0:T(8,128)(2,1)}, u32[]{:S(2)}) copy-start(bf16[8320,128]{1,0:T(8,128)(2,1)} %reshape.166) | copy-start | bytes 6389764
  200.4 5.0 %copy-start = (bf16[384,8320]{1,0:T(8,128)(2,1)S(1)}, bf16[384,8320]{1,0:T(8,128)(2,1)}, u32[]{:S(2)}) copy-start(bf16[384,8320]{1,0:T(8,128)(2,1)} %copy.29) | copy-start | bytes 19169284
  200.4 5.3 %copy-start.9 = (bf16[8320,128]{1,0:T(8,128)(2,1)S(1)}, bf16[8320,128]{1,0:T(8,128)(2,1)}, u32[]{:S(2)}) copy-start(bf16[8320,128]{1,0:T(8,128)(2,1)} %reshape.164) | copy-start | bytes 6389764
  205.7 2.0 copy-start.8
  207.7 2.0 copy-start.7
  209.7 2.0 copy-start.6
  211.7 2.0 copy-start.4
  213.7 2.0 copy-start.3
  215.8 2.0 copy-start.2
  217.8 2.0 copy-start.11
  221.8 65.7 %copy-start.24 = (f32[128]{0:T(128)S(1)}, f32[128]{0:T(128)}, u32[]{:S(2)}) copy-start(f32[128]{0:T(128)} %get-tuple-element.6) | copy-start | bytes 1540
  222.0 1.2 copy-start.12
  223.2 130.6 %all-reduce.10.cloned.1.call-start = ((), (), s32[]{:S(2)}) async-start(), calls=%async_computation.1 | async-start | bytes 3538944 | tf_op jit(solution)/shard_map/psum | solution.py:11
Sparse Core Ops, SparseCore 0:
  223.3 64.0 all-reduce.7
  290.6 63.2 all-reduce.9
